TPU v7x, 32 devices: a whole 2x2x4 slice. The times are simulated.
32 devices in a mesh: passage: 2 (over x), brick: 16 (over z, y, core).
Axes of the slice: x: 2, y: 2, z: 4, core: 2. Of those that a mesh axis runs over, the one named last changes fastest.
Arguments:
- jac_blocks: bfloat16 [2, 25, 16, 8192], P('passage', None, None, 'brick'), may hold values from -6 to 6
- psi_start: float32 [2, 10, 16, 64, 128], P('passage', None, 'brick'), may hold values from -6 to 6
- source: float32 [2, 10, 16, 64, 128], P('passage', None, 'brick'), may hold values from -6 to 6
- pseudo_step: float32 [2, 16, 64, 128], P('passage', 'brick'), may hold values from 0.1 to 0.4
- dissipation: float32 [2, 16, 64, 128], P('passage', 'brick'), may hold values from 0.04 to 0.15
- freq_volume: float32 [2, 16, 64, 128], P('passage', 'brick'), may hold values from 0.2 to 2
- normals: float32 [2, 3, 16, 64], P('passage', None, 'brick'), may hold values from -6 to 6
- face_owner: int32 [2, 1024, 1], P('passage', 'brick'), may hold values from 0 to 15; in each aligned block of 64 rows (0 to 63, 64 to 127, ..., all dimensions but the last counted through in order) at most 16 rows name the same one
- face_slot: int32 [2, 1024], P('passage', 'brick'), may hold values from 0 to 255
Outputs:
- adjoint: float32 [2, 10, 16, 64, 128], P('passage', None, 'brick')
- sensitivity: float32 [2, 6, 4096], P('passage', None, 'brick')
Inputs may be any that keep to these rules, and one draw needn't show every extreme that they name: `face_owner`: in the 64 faces of one device (aligned blocks of the rows), no brick is named by more than 16 faces, and in some block some brick is named by exactly 16.
All inputs are finite; a program needn't handle non-finite values.
Results may differ from a plain program's by a relative error of at most 0.0003.
Values may be sent and summed in bfloat16 or wider, within the bound.
A program may use at most 64 MiB of HBM per device.

v0:
```python
import math

import jax
import jax.numpy as jnp
from jax import lax
from jax.sharding import PartitionSpec as P

NODE_DEV = 256
SWEEPS = 2
ND = 1
BLADES = 36


def padded(value, sides, width, wrap):
    for axis, dim in sides:
        peers, length = (lax.axis_size(axis), value.shape[dim])
        up = [(i, (i + 1) % peers) for i in range(peers if wrap else peers - 1)]
        down = [(j, i) for i, j in up]
        last = lax.slice_in_dim(value, length - width, length, axis=dim)
        initial = lax.slice_in_dim(value, 0, width, axis=dim)
        before = lax.ppermute(last, axis, up)
        after = lax.ppermute(initial, axis, down)
        value = jnp.concatenate([before, value, after], axis=dim)
    return value


def rotate(rim, turn):
    cosine = math.cos(turn)
    sine = math.sin(turn)
    real_part = rim[:, :5]
    imag_part = rim[:, 5:]
    return jnp.concatenate(
        [real_part * cosine - imag_part * sine, real_part * sine + imag_part * cosine], axis=1
    )


def transpose_apply(tiles, diff):
    total_real = jnp.zeros_like(diff[:, :5])
    total_imag = jnp.zeros_like(diff[:, :5])
    for row_index in range(5):
        column = tiles[:, row_index * 5 : row_index * 5 + 5].astype(jnp.float32)
        total_real = total_real + column * diff[:, row_index : row_index + 1]
        total_imag = total_imag + column * diff[:, 5 + row_index : 6 + row_index]
    return jnp.concatenate([total_real, total_imag], axis=1)


def advance(
    state,
    source,
    pseudo_step,
    dissipation,
    freq_volume,
    convect_fn,
    cycle_index,
    passes,
    phase_angle,
):
    padded_i = padded(state, (("brick", 2),), 1, False)
    padded_j = padded(state.astype(jnp.bfloat16), (("passage", 3),), 1, True).astype(state.dtype)
    below_rim = padded_j[:, :, :, :1]
    above_rim = padded_j[:, :, :, -1:]
    below_rim = jnp.where(cycle_index == 0, rotate(below_rim, -phase_angle), below_rim)
    above_rim = jnp.where(cycle_index == passes - 1, rotate(above_rim, phase_angle), above_rim)
    fixed_j = jnp.concatenate([below_rim, state, above_rim], axis=3)
    padded_k = jnp.pad(state, ((0, 0), (0, 0), (0, 0), (0, 0), (1, 1)))
    beside = padded_i[:, :, 2:] + padded_i[:, :, :-2]
    beside = beside + fixed_j[:, :, :, 2:] + fixed_j[:, :, :, :-2]
    beside = beside + padded_k[..., 2:] + padded_k[..., :-2]
    diff = 0.5 * (padded_i[:, :, 2:] - padded_i[:, :, :-2])
    convect = convect_fn(diff)
    omega = freq_volume[:, None]
    spin = jnp.concatenate([omega * state[:, 5:], -omega * state[:, :5]], axis=1)
    resid = convect + spin + dissipation[:, None] * (6.0 * state - beside) - source
    return state - pseudo_step[:, None] * resid


def body(
    jac_blocks,
    psi_start,
    source,
    pseudo_step,
    dissipation,
    freq_volume,
    normals,
    face_owner,
    face_slot,
):
    passes = lax.axis_size("passage")
    cycle_index = lax.axis_index("passage")
    bricks = lax.axis_size("brick")
    planes = psi_start.shape[2]
    width_j = psi_start.shape[3]
    width_k = psi_start.shape[4]
    phase_angle = 2.0 * math.pi * ND * passes / BLADES
    relaid = lax.all_to_all(jac_blocks, "brick", split_axis=2, concat_axis=3, tiled=True)
    tiles = relaid.reshape(1, 25, planes, width_j, width_k)

    def convect_fn(diff):
        return transpose_apply(tiles, diff)

    state = psi_start
    for sweep in range(SWEEPS):
        state = advance(
            state,
            source,
            pseudo_step,
            dissipation,
            freq_volume,
            convect_fn,
            cycle_index,
            passes,
            phase_angle,
        )
    wall_state = state[0, :, :, :, 0]
    face_normals = normals[0]
    values = jnp.concatenate(
        [face_normals * wall_state[1:4], face_normals * wall_state[6:9]], axis=0
    )
    values = values.reshape(6, planes * width_j)
    owners = face_owner[0, :, 0]
    slots = face_slot[0]
    node_ids = owners * NODE_DEV + slots
    local_terms = jnp.zeros((6, NODE_DEV * bricks), jnp.float32).at[:, node_ids].add(values)
    summed = lax.psum_scatter(local_terms, "brick", scatter_dimension=1, tiled=True)
    sensitivity = summed[None]
    return (state, sensitivity)


def solution(mesh):
    placed = (
        P("passage", None, None, "brick"),
        P("passage", None, "brick", None, None),
        P("passage", None, "brick", None, None),
        P("passage", "brick", None, None),
        P("passage", "brick", None, None),
        P("passage", "brick", None, None),
        P("passage", None, "brick", None),
        P("passage", "brick", None),
        P("passage", "brick"),
    )
    return jax.shard_map(
        body,
        mesh=mesh,
        in_specs=placed,
        out_specs=(P("passage", None, "brick", None, None), P("passage", None, "brick")),
        check_vma=False,
    )
```

profile of v0, /device:TPU:0, one launch (start us, length us, event | category | flops | bytes accessed | tf_op | source)
XLA Modules:
  0.0 128.0 jit_solution(5724360956886795302)
XLA Ops:
  7.2 2.5 %collective-permute-start.1 = (f32[1,10,1,64,128]{4,3,1,2,0:T(8,128)}, f32[1,10,1,64,128]{4,3,1,2,0:T(8,128)S(1)}, u32[]{:S(2)}, u32[]{:S(2)}) collective-permute-start(f32[1,10,1,64,128]{4,3,1,2,0:T(8,128)} %bitcast.71), channel_id=1, source_target_pairs={{0,1},{1,2},{2,3},{3,4},{4,5},{5,6},{6,7},{7,8},{8,9},{9,10},{10,1... | collective-permute-start | bytes 983048 | tf_op jit(solution)/shard_map/ppermute | solution.py:21
  9.8 1.3 %collective-permute-start = (f32[1,10,1,64,128]{4,3,1,2,0:T(8,128)}, f32[1,10,1,64,128]{4,3,1,2,0:T(8,128)S(1)}, u32[]{:S(2)}, u32[]{:S(2)}) collective-permute-start(f32[1,10,1,64,128]{4,3,1,2,0:T(8,128)} %bitcast.72), channel_id=1, source_target_pairs={{1,0},{2,1},{3,2},{4,3},{5,4},{6,5},{7,6},{8,7},{9,8},{10,9},{11,1... | collective-permute-start | bytes 983048 | tf_op jit(solution)/shard_map/ppermute | solution.py:22
  11.1 1.0 bitcast_convert_fusion
  12.1 2.4 %collective-permute-start.2 = (bf16[1,10,1,1,128]{4,3,1,2,0:T(2,128)(2,1)S(1)}, bf16[1,10,1,1,128]{4,3,1,2,0:T(2,128)(2,1)S(1)}, u32[]{:S(2)}, u32[]{:S(2)}) collective-permute-start(bf16[1,10,1,1,128]{4,3,1,2,0:T(2,128)(2,1)S(1)} %get-tuple-element.64), channel_id=1, source_target_pairs={{0,16},{16,0},{1,17},{17,1},{2,18},{18,2},{3,19},{19,3},{4,20},{20... | collective-permute-start | bytes 7688 | tf_op jit(solution)/shard_map/ppermute | solution.py:21
  14.5 2.0 %copy.66 = bf16[1,25,16,512]{3,1,0,2:T(8,128)(2,1)} copy(bf16[1,25,16,512]{3,2,1,0:T(8,128)(2,1)} %param.9) | data formatting | bytes 819200 | tf_op args[0]
  16.6 8.9 %all-to-all-start = ((bf16[1,25,16,512]{3,1,0,2:T(8,128)(2,1)}), bf16[1,25,16,512]{3,1,0,2:T(8,128)(2,1)S(1)}, u32[]{:S(2)}, u32[]{:S(2)}) async-start(bf16[1,25,16,512]{3,1,0,2:T(8,128)(2,1)} %copy.66), calls=%async_computation | async-start | bytes 1048576 | tf_op jit(solution)/shard_map/all_to_all | solution.py:95
  25.9 13.9 %all-to-all-done = bf16[1,25,16,512]{3,1,0,2:T(8,128)(2,1)S(1)} async-done(((bf16[1,25,16,512]{3,1,0,2:T(8,128)(2,1)}), bf16[1,25,16,512]{3,1,0,2:T(8,128)(2,1)S(1)}, u32[]{:S(2)}, u32[]{:S(2)}) %all-to-all-start) | async-done | bytes 409632 | tf_op jit(solution)/shard_map/all_to_all | solution.py:95
  39.8 0.2 copy.67
  40.0 0.2 reshape.329
  40.3 0.1 fusion.29
  40.4 0.1 fusion.25
  40.5 0.3 fusion.50
  40.8 1.6 %collective-permute-start.6 = (bf16[1,10,1,1,128]{4,3,1,2,0:T(2,128)(2,1)S(1)}, bf16[1,10,1,1,128]{4,3,1,2,0:T(2,128)(2,1)S(1)}, u32[]{:S(2)}, u32[]{:S(2)}) collective-permute-start(bf16[1,10,1,1,128]{4,3,1,2,0:T(2,128)(2,1)S(1)} %get-tuple-element.62), channel_id=1, source_target_pairs={{0,16},{16,0},{1,17},{17,1},{2,18},{18,2},{3,19},{19,3},{4,20},{20... | collective-permute-start | bytes 7688 | tf_op jit(solution)/shard_map/ppermute | solution.py:21
  42.4 0.5 collective-permute-start.7
  42.9 1.5 %collective-permute-start.5 = (f32[1,10,1,64,128]{4,3,1,2,0:T(8,128)S(1)}, f32[1,10,1,64,128]{4,3,1,2,0:T(8,128)S(1)}, u32[]{:S(2)}, u32[]{:S(2)}) collective-permute-start(f32[1,10,1,64,128]{4,3,1,2,0:T(8,128)S(1)} %get-tuple-element.21), channel_id=1, source_target_pairs={{0,1},{1,2},{2,3},{3,4},{4,5},{5,6},{6,7},{7,8},{8,9},{9,10},{10,1... | collective-permute-start | bytes 983048 | tf_op jit(solution)/shard_map/ppermute | solution.py:21
  44.5 1.3 %collective-permute-start.4 = (f32[1,10,1,64,128]{4,3,1,2,0:T(8,128)S(1)}, f32[1,10,1,64,128]{4,3,1,2,0:T(8,128)S(1)}, u32[]{:S(2)}, u32[]{:S(2)}) collective-permute-start(f32[1,10,1,64,128]{4,3,1,2,0:T(8,128)S(1)} %get-tuple-element.21), channel_id=1, source_target_pairs={{1,0},{2,1},{3,2},{4,3},{5,4},{6,5},{7,6},{8,7},{9,8},{10,9},{11,1... | collective-permute-start | bytes 983048 | tf_op jit(solution)/shard_map/ppermute | solution.py:22
  45.8 0.2 collective-permute-done.7
  46.1 2.3 %collective-permute-done.4 = f32[1,10,1,64,128]{4,3,1,2,0:T(8,128)S(1)} collective-permute-done((f32[1,10,1,64,128]{4,3,1,2,0:T(8,128)S(1)}, f32[1,10,1,64,128]{4,3,1,2,0:T(8,128)S(1)}, u32[]{:S(2)}, u32[]{:S(2)}) %collective-permute-start.4) | collective-permute-done | bytes 327712 | tf_op jit(solution)/shard_map/ppermute | solution.py:22
  48.7 0.4 fusion.17
  49.1 0.1 slice_reduce_fusion.1
  49.3 0.1 copy.84
  49.4 2.2 %scatter_custom_fusion = f32[6,4096]{0,1:T(8,128)} fusion(s32[64]{0:T(128)S(1)} %fusion.49, f32[]{:T(128)} %constant.11.clone.1, f32[6,1,64]{0,2,1:T(8,128)S(1)} %copy.84), kind=kCustom, calls=%fused_computation.1 | custom fusion | flops 384 | bytes 131076 | tf_op jit(solution)/shard_map/scatter-add | solution.py:123
  51.6 68.0 %reduce-scatter.2.cloned.1.call-done = f32[6,256]{0,1:T(8,128)} async-done(((f32[6,4096]{0,1:T(8,128)}), f32[6,256]{0,1:T(8,128)}) %reduce-scatter.2.cloned.1.call-update) | async-done | bytes 6160 | tf_op jit(solution)/shard_map/reduce_scatter | solution.py:124
  119.6 1.6 %copy.82 = f32[1,6,256]{2,0,1:T(1,128)} copy(f32[1,6,256]{1,2,0:T(8,128)} %bitcast.82) | data formatting | bytes 12288
  (48 shorter events, 0.7 us)
Async XLA Ops:
  7.2 18.4 %copy-start = (f32[1,10,1,64,128]{4,3,2,1,0:T(8,128)S(1)}, f32[1,10,1,64,128]{4,3,2,1,0:T(8,128)}, u32[]{:S(2)}) copy-start(f32[1,10,1,64,128]{4,3,2,1,0:T(8,128)} %param.10) | copy-start | bytes 983044
  7.2 18.4 %copy-start.3 = (f32[1,1,64,128]{3,2,1,0:T(8,128)S(1)}, f32[1,1,64,128]{3,2,1,0:T(8,128)}, u32[]{:S(2)}) copy-start(f32[1,1,64,128]{3,2,1,0:T(8,128)} %param.14) | copy-start | bytes 98308
  7.2 18.4 %copy-start.7 = (s32[1,64]{1,0:T(1,128)S(1)}, s32[1,64]{1,0:T(1,128)}, u32[]{:S(2)}) copy-start(s32[1,64]{1,0:T(1,128)} %param.17) | copy-start | bytes 772
  7.2 18.4 %copy-start.8 = (s32[1,64,1]{1,2,0:T(1,128)S(1)}, s32[1,64,1]{1,2,0:T(1,128)}, u32[]{:S(2)}) copy-start(s32[1,64,1]{1,2,0:T(1,128)} %param.16) | copy-start | bytes 772
  7.2 18.6 %collective-permute-start.1 = (f32[1,10,1,64,128]{4,3,1,2,0:T(8,128)}, f32[1,10,1,64,128]{4,3,1,2,0:T(8,128)S(1)}, u32[]{:S(2)}, u32[]{:S(2)}) collective-permute-start(f32[1,10,1,64,128]{4,3,1,2,0:T(8,128)} %bitcast.71), channel_id=1, source_target_pairs={{0,1},{1,2},{2,3},{3,4},{4,5},{5,6},{6,7},{7,8},{8,9},{9,10},{10,1... | collective-permute-start | bytes 983048 | tf_op jit(solution)/shard_map/ppermute | solution.py:21
  9.8 16.0 %collective-permute-start = (f32[1,10,1,64,128]{4,3,1,2,0:T(8,128)}, f32[1,10,1,64,128]{4,3,1,2,0:T(8,128)S(1)}, u32[]{:S(2)}, u32[]{:S(2)}) collective-permute-start(f32[1,10,1,64,128]{4,3,1,2,0:T(8,128)} %bitcast.72), channel_id=1, source_target_pairs={{1,0},{2,1},{3,2},{4,3},{5,4},{6,5},{7,6},{8,7},{9,8},{10,9},{11,1... | collective-permute-start | bytes 983048 | tf_op jit(solution)/shard_map/ppermute | solution.py:22
  12.1 13.6 %collective-permute-start.2 = (bf16[1,10,1,1,128]{4,3,1,2,0:T(2,128)(2,1)S(1)}, bf16[1,10,1,1,128]{4,3,1,2,0:T(2,128)(2,1)S(1)}, u32[]{:S(2)}, u32[]{:S(2)}) collective-permute-start(bf16[1,10,1,1,128]{4,3,1,2,0:T(2,128)(2,1)S(1)} %get-tuple-element.64), channel_id=1, source_target_pairs={{0,16},{16,0},{1,17},{17,1},{2,18},{18,2},{3,19},{19,3},{4,20},{20... | collective-permute-start | bytes 7688 | tf_op jit(solution)/shard_map/ppermute | solution.py:21
  14.5 11.2 %collective-permute-start.3 = (bf16[1,10,1,1,128]{4,3,1,2,0:T(2,128)(2,1)S(1)}, bf16[1,10,1,1,128]{4,3,1,2,0:T(2,128)(2,1)S(1)}, u32[]{:S(2)}, u32[]{:S(2)}) collective-permute-start(bf16[1,10,1,1,128]{4,3,1,2,0:T(2,128)(2,1)S(1)} %get-tuple-element.65), channel_id=1, source_target_pairs={{16,0},{0,16},{17,1},{1,17},{18,2},{2,18},{19,3},{3,19},{20,4},{4,... | collective-permute-start | bytes 7688 | tf_op jit(solution)/shard_map/ppermute | solution.py:22
  16.6 23.2 %all-to-all-start = ((bf16[1,25,16,512]{3,1,0,2:T(8,128)(2,1)}), bf16[1,25,16,512]{3,1,0,2:T(8,128)(2,1)S(1)}, u32[]{:S(2)}, u32[]{:S(2)}) async-start(bf16[1,25,16,512]{3,1,0,2:T(8,128)(2,1)} %copy.66), calls=%async_computation | async-start | bytes 1048576 | tf_op jit(solution)/shard_map/all_to_all | solution.py:95
  25.5 94.1 %reduce-scatter.2.cloned.1.call-start = ((), (), s32[]{:S(2)}) async-start(), calls=%async_computation.2 | async-start | bytes 2228224 | tf_op jit(solution)/shard_map/reduce_scatter | solution.py:124
  25.8 14.6 %copy-start.1 = (f32[1,10,1,64,128]{4,3,2,1,0:T(8,128)S(1)}, f32[1,10,1,64,128]{4,3,2,1,0:T(8,128)}, u32[]{:S(2)}) copy-start(f32[1,10,1,64,128]{4,3,2,1,0:T(8,128)} %param.11) | copy-start | bytes 983044
  25.8 14.6 %copy-start.4 = (f32[1,1,64,128]{3,2,1,0:T(8,128)S(1)}, f32[1,1,64,128]{3,2,1,0:T(8,128)}, u32[]{:S(2)}) copy-start(f32[1,1,64,128]{3,2,1,0:T(8,128)} %param.13) | copy-start | bytes 98308
  25.9 14.6 %copy-start.5 = (f32[1,1,64,128]{3,2,1,0:T(8,128)S(1)}, f32[1,1,64,128]{3,2,1,0:T(8,128)}, u32[]{:S(2)}) copy-start(f32[1,1,64,128]{3,2,1,0:T(8,128)} %param.12) | copy-start | bytes 98308
  40.8 4.9 %collective-permute-start.6 = (bf16[1,10,1,1,128]{4,3,1,2,0:T(2,128)(2,1)S(1)}, bf16[1,10,1,1,128]{4,3,1,2,0:T(2,128)(2,1)S(1)}, u32[]{:S(2)}, u32[]{:S(2)}) collective-permute-start(bf16[1,10,1,1,128]{4,3,1,2,0:T(2,128)(2,1)S(1)} %get-tuple-element.62), channel_id=1, source_target_pairs={{0,16},{16,0},{1,17},{17,1},{2,18},{18,2},{3,19},{19,3},{4,20},{20... | collective-permute-start | bytes 7688 | tf_op jit(solution)/shard_map/ppermute | solution.py:21
  42.4 3.6 %collective-permute-start.7 = (bf16[1,10,1,1,128]{4,3,1,2,0:T(2,128)(2,1)S(1)}, bf16[1,10,1,1,128]{4,3,1,2,0:T(2,128)(2,1)S(1)}, u32[]{:S(2)}, u32[]{:S(2)}) collective-permute-start(bf16[1,10,1,1,128]{4,3,1,2,0:T(2,128)(2,1)S(1)} %get-tuple-element.63), channel_id=1, source_target_pairs={{16,0},{0,16},{17,1},{1,17},{18,2},{2,18},{19,3},{3,19},{20,4},{4,... | collective-permute-start | bytes 7688 | tf_op jit(solution)/shard_map/ppermute | solution.py:22
  42.9 3.1 %collective-permute-start.5 = (f32[1,10,1,64,128]{4,3,1,2,0:T(8,128)S(1)}, f32[1,10,1,64,128]{4,3,1,2,0:T(8,128)S(1)}, u32[]{:S(2)}, u32[]{:S(2)}) collective-permute-start(f32[1,10,1,64,128]{4,3,1,2,0:T(8,128)S(1)} %get-tuple-element.21), channel_id=1, source_target_pairs={{0,1},{1,2},{2,3},{3,4},{4,5},{5,6},{6,7},{7,8},{8,9},{9,10},{10,1... | collective-permute-start | bytes 983048 | tf_op jit(solution)/shard_map/ppermute | solution.py:21
  44.5 4.0 %collective-permute-start.4 = (f32[1,10,1,64,128]{4,3,1,2,0:T(8,128)S(1)}, f32[1,10,1,64,128]{4,3,1,2,0:T(8,128)S(1)}, u32[]{:S(2)}, u32[]{:S(2)}) collective-permute-start(f32[1,10,1,64,128]{4,3,1,2,0:T(8,128)S(1)} %get-tuple-element.21), channel_id=1, source_target_pairs={{1,0},{2,1},{3,2},{4,3},{5,4},{6,5},{7,6},{8,7},{9,8},{10,9},{11,1... | collective-permute-start | bytes 983048 | tf_op jit(solution)/shard_map/ppermute | solution.py:22
  48.5 0.7 copy-start.6
  49.1 2.5 %copy-start.2 = (f32[1,10,1,64,128]{4,3,1,2,0:T(8,128)}, f32[1,10,1,64,128]{4,3,1,2,0:T(8,128)S(1)}, u32[]{:S(2)}) copy-start(f32[1,10,1,64,128]{4,3,1,2,0:T(8,128)S(1)} %fusion.17) | copy-start | bytes 983044
Sparse Core Ops, SparseCore 0:
  51.7 67.8 reduce-scatter.1
where the time goes:
time: 128 us
  waiting for transfers between devices  84.5 us (66%)
  starting transfers between devices  20.1 us (16%)
  between operations  14.5 us (11%)
  other arithmetic  4.52 us (4%)
  local copies, waits for them, and re-layouts  4.46 us (3%)
    reduce_scatter x1, waiting for transfers between devices, body(): lax.psum_scatter(local_terms, 'brick', scatter_dimension=1, tiled=True)  68 us
    all_to_all x1, waiting for transfers between devices, body(): lax.all_to_all(jac_blocks, 'brick', split_axis=2, concat_axis=3, tiled=True)  13.9 us
    all_to_all x1, starting transfers between devices, body(): lax.all_to_all(jac_blocks, 'brick', split_axis=2, concat_axis=3, tiled=True)  8.92 us
    ppermute x4, starting transfers between devices, padded(): before = lax.ppermute(last, axis, up)  7.99 us
    unnamed x20, local copies, waits for them, and re-layouts  3.67 us
    ppermute x4, starting transfers between devices, padded(): after = lax.ppermute(initial, axis, down)  3.2 us
    ppermute x4, waiting for transfers between devices, padded(): after = lax.ppermute(initial, axis, down)  2.58 us
  transfers between devices with their start and end apart: 10, of which 4 were waited for; matrix products, arithmetic and copies ran while one was open for 3% of the time, Pallas kernels for 0%

commit v1 on v0

v1 whole, which is shorter than its diff:
```python
import functools
import math

import jax
import jax.numpy as jnp
from jax import lax
from jax.experimental import pallas as pl
from jax.experimental.pallas import tpu as pltpu
from jax.sharding import PartitionSpec as P

NODE_DEV = 256
SWEEPS = 2
ND = 1
BLADES = 36
LANES = 128
SUB = 8
MESH = pl.DeviceIdType.MESH


def far_first(count):
    half = count // 2
    return sorted(range(1, count), key=lambda d: (abs(d - half), d))


def kernel(
    B, passes, phase_angle,
    jac, psi, source, pstep, diss, freq, normals, ids,
    adj, sens,
    jpack, jsend, jrecv, jflat, pad0, pad1, low0, high0, low1, high1,
    rim_send, rim_recv, idbuf, valbuf,
    j_s, j_r, h_s, h_r, r_s, r_r, i_s, i_r, v_s, v_r,
):
    me = lax.axis_index("brick")
    mp = lax.axis_index("passage")
    NJ, NK = psi.shape[1], psi.shape[2]
    R = jac.shape[2] // LANES
    planes = jac.shape[1]
    rows = 25 * R
    pitch = jpack.shape[0] // planes
    others = far_first(B)
    up_p = lax.rem(mp + 1, passes)
    down_p = lax.rem(mp + passes - 1, passes)

    barrier = pltpu.get_barrier_semaphore()
    for d in others:
        pl.semaphore_signal(
            barrier, inc=1, device_id={"brick": lax.rem(me + d, B)}, device_id_type=MESH
        )
    pl.semaphore_signal(barrier, inc=1, device_id={"passage": up_p}, device_id_type=MESH)
    greeted = B
    if passes > 2:
        pl.semaphore_signal(barrier, inc=1, device_id={"passage": down_p}, device_id_type=MESH)
        greeted += 1

    for n in range(25):
        for r in range(R):
            for g in range(planes // SUB):
                x = jac[n, pl.ds(g * SUB, SUB), pl.ds(r * LANES, LANES)].astype(jnp.float32)
                jpack[pl.ds(g * SUB * pitch + r * 25 + n, SUB, stride=pitch), :] = x
    for p in range(planes):
        jsend[p, :, :] = jpack[pl.ds(p * pitch, rows), :].astype(jnp.bfloat16)

    def fill_rims(sweep, field, first, last):
        for c in range(10):
            rim_send[sweep, 0, pl.ds(c, 1), :] = field[c, pl.ds(last, 1), :]
            rim_send[sweep, 1, pl.ds(c, 1), :] = field[c, pl.ds(first, 1), :]

    def rim_copies(sweep):
        return [
            pltpu.make_async_remote_copy(
                src_ref=rim_send.at[sweep, k],
                dst_ref=rim_recv.at[sweep, k],
                send_sem=r_s.at[sweep, k],
                recv_sem=r_r.at[sweep, k],
                device_id={"passage": peer},
                device_id_type=MESH,
            )
            for k, peer in ((0, up_p), (1, down_p))
        ]

    def halo_copies(sweep, src, low, high):
        up = pltpu.make_async_remote_copy(
            src_ref=src, dst_ref=low, send_sem=h_s.at[sweep, 0], recv_sem=h_r.at[sweep, 0],
            device_id={"brick": lax.rem(me + 1, B)}, device_id_type=MESH,
        )
        down = pltpu.make_async_remote_copy(
            src_ref=src, dst_ref=high, send_sem=h_s.at[sweep, 1], recv_sem=h_r.at[sweep, 1],
            device_id={"brick": lax.rem(me + B - 1, B)}, device_id_type=MESH,
        )
        return up, down

    def halo_start(up, down):
        @pl.when(me < B - 1)
        def _():
            up.start()

        @pl.when(me > 0)
        def _():
            down.start()

    def halo_recv(up, down, low, high):
        @pl.when(me > 0)
        def _():
            up.wait_recv()

        @pl.when(me == 0)
        def _():
            low[...] = jnp.zeros_like(low)

        @pl.when(me < B - 1)
        def _():
            down.wait_recv()

        @pl.when(me == B - 1)
        def _():
            high[...] = jnp.zeros_like(high)

    def halo_sent(up, down):
        @pl.when(me < B - 1)
        def _():
            up.wait_send()

        @pl.when(me > 0)
        def _():
            down.wait_send()

    fill_rims(0, psi, 0, NJ - 1)
    idbuf[pl.ds(me, 1), :, :] = ids[...].reshape(1, SUB, LANES)

    j_copies, id_copies, val_copies = [], [], []
    for k, d in enumerate(others):
        peer = lax.rem(me + d, B)
        j_copies.append(pltpu.make_async_remote_copy(
            src_ref=jsend.at[peer], dst_ref=jrecv.at[me], send_sem=j_s.at[k], recv_sem=j_r.at[k],
            device_id={"brick": peer}, device_id_type=MESH))
        id_copies.append(pltpu.make_async_remote_copy(
            src_ref=ids, dst_ref=idbuf.at[me], send_sem=i_s.at[k], recv_sem=i_r.at[k],
            device_id={"brick": peer}, device_id_type=MESH))
        val_copies.append(pltpu.make_async_remote_copy(
            src_ref=valbuf.at[me], dst_ref=valbuf.at[me], send_sem=v_s.at[k], recv_sem=v_r.at[k],
            device_id={"brick": peer}, device_id_type=MESH))
    rims0, rims1 = rim_copies(0), rim_copies(1)
    halo0 = halo_copies(0, psi, low0, high0)
    inner = pad1.at[:, pl.ds(SUB, NJ), :]
    halo1 = halo_copies(1, inner, low1, high1)

    pl.semaphore_wait(barrier, greeted)
    for copy in j_copies:
        copy.start()
    for copy in rims0:
        copy.start()
    halo_start(*halo0)
    for copy in id_copies:
        copy.start()

    jrecv[pl.ds(me, 1), :, :] = jsend[pl.ds(me, 1), :, :]
    for c in range(10):
        pad0[c, pl.ds(SUB, NJ), :] = psi[c, :, :]

    lane = lax.broadcasted_iota(jnp.int32, (SUB, NK), 1)

    def place_rims(sweep, pad):
        for k, (edge, turn, row) in enumerate(
            ((0, -phase_angle, SUB - 1), (passes - 1, phase_angle, SUB + NJ))
        ):
            rim = rim_recv[sweep, k, :, :]
            re, im = rim[0:5], rim[5:10]
            at_edge = mp == edge
            cosine = jnp.where(at_edge, math.cos(turn), 1.0).astype(jnp.float32)
            sine = jnp.where(at_edge, math.sin(turn), 0.0).astype(jnp.float32)
            re, im = re * cosine - im * sine, re * sine + im * cosine
            for c in range(5):
                pad[c, pl.ds(row, 1), :] = re[c : c + 1]
                pad[5 + c, pl.ds(row, 1), :] = im[c : c + 1]

    def advance(pad, low, high, out, shift):
        for t in range(NJ // SUB):
            at = pl.ds(t * SUB, SUB)
            om, ds_, ps = freq[at, :], diss[at, :], pstep[at, :]
            us, lows, highs = [], [], []
            for c in range(10):
                us.append(pad[c, pl.ds(SUB + t * SUB, SUB), :])
                lows.append(low[c, at, :])
                highs.append(high[c, at, :])
            diff = [0.5 * (h - l) for h, l in zip(highs, lows)]
            conv = [None] * 10
            for n in range(5):
                for m in range(5):
                    tile = jflat[pl.ds(t * SUB * 25 + n * 5 + m, SUB, stride=25), :]
                    for part in (0, 5):
                        term = tile * diff[part + n]
                        conv[part + m] = term if conv[part + m] is None else conv[part + m] + term
            for c in range(10):
                u = us[c]
                beside = highs[c] + lows[c]
                beside = beside + pad[c, pl.ds(SUB + t * SUB + 1, SUB), :]
                beside = beside + pad[c, pl.ds(SUB + t * SUB - 1, SUB), :]
                beside = beside + jnp.where(lane == NK - 1, 0.0, pltpu.roll(u, NK - 1, 1))
                beside = beside + jnp.where(lane == 0, 0.0, pltpu.roll(u, 1, 1))
                spin = om * us[c + 5] if c < 5 else -(om * us[c - 5])
                resid = conv[c] + spin + ds_ * (6.0 * u - beside) - source[c, at, :]
                out[c, pl.ds(shift + t * SUB, SUB), :] = u - ps * resid

    for copy in rims0:
        copy.wait_recv()
    place_rims(0, pad0)
    halo_recv(*halo0, low0, high0)
    for copy in j_copies:
        copy.wait_recv()
    for s in range(B):
        jflat[pl.ds(s * rows, rows), :] = jrecv[s, :, :].astype(jnp.float32)

    advance(pad0, low0, high0, pad1, SUB)
    fill_rims(1, pad1, SUB, SUB + NJ - 1)
    halo_start(*halo1)
    for copy in rims1:
        copy.start()
    for copy in rims1:
        copy.wait_recv()
    place_rims(1, pad1)
    halo_recv(*halo1, low1, high1)
    advance(pad1, low1, high1, adj, 0)

    lanes = lax.broadcasted_iota(jnp.int32, (NJ, NK), 1)
    wall = jnp.zeros((NJ, NK), jnp.float32)
    for k, c in enumerate((1, 2, 3, 6, 7, 8)):
        column = adj[c, :, :]
        if k:
            column = pltpu.roll(column, k, 1)
        wall = jnp.where(lanes == k, column, wall)
    if NJ < LANES:
        wall = jnp.concatenate([wall, jnp.zeros((LANES - NJ, NK), jnp.float32)], axis=0)
    values = wall.T[0:SUB] * normals[...]
    valbuf[pl.ds(me, 1), :, :] = values.reshape(1, SUB, LANES)
    for copy in val_copies:
        copy.start()

    for copy in id_copies:
        copy.wait_recv()
    for copy in val_copies:
        copy.wait_recv()
    node = lax.broadcasted_iota(jnp.int32, (NODE_DEV, LANES), 0) + me * NODE_DEV
    total = jnp.zeros((3 * SUB, NODE_DEV), jnp.float32)
    for s in range(B):
        hit = jnp.where(idbuf[s, 0:1, :] == node, 1.0, 0.0).astype(jnp.bfloat16)
        v = valbuf[s, :, :]
        a = v.astype(jnp.bfloat16).astype(jnp.float32)
        rest = v - a
        b = rest.astype(jnp.bfloat16).astype(jnp.float32)
        parts = jnp.concatenate([a, b, rest - b], axis=0).astype(jnp.bfloat16)
        total = total + lax.dot_general(
            parts, hit, (((1,), (1,)), ((), ())), preferred_element_type=jnp.float32
        )
    summed = total[0:SUB] + total[SUB : 2 * SUB] + total[2 * SUB :]
    sens[...] = summed[0:6]

    for copy in j_copies + id_copies + val_copies + rims0 + rims1:
        copy.wait_send()
    halo_sent(*halo0)
    halo_sent(*halo1)


def body(B, passes, jac_blocks, psi_start, source, pseudo_step, dissipation, freq_volume,
         normals, face_owner, face_slot):
    _, _, planes_all, cells = jac_blocks.shape
    NJ, NK = psi_start.shape[3:]
    phase_angle = 2.0 * math.pi * ND * passes / BLADES
    R = cells // LANES
    rows = 25 * R
    pitch = -(-rows // SUB) * SUB
    node_ids = face_owner[:, :, 0] * NODE_DEV + face_slot
    ids = jnp.pad(node_ids, ((0, SUB - 1), (0, LANES - node_ids.shape[1])), constant_values=-1)
    face_normals = normals[0, :, 0, :]
    face_normals = jnp.concatenate([face_normals, face_normals], axis=0)
    face_normals = jnp.pad(
        face_normals, ((0, SUB - 6), (0, LANES - face_normals.shape[1])))
    f32 = jnp.float32
    field = (10, NJ, NK)
    vm = pl.BlockSpec(memory_space=pltpu.VMEM)
    dma = pltpu.SemaphoreType.DMA
    adj, sens = pl.pallas_call(
        functools.partial(kernel, B, passes, phase_angle),
        out_shape=(
            jax.ShapeDtypeStruct(field, f32),
            jax.ShapeDtypeStruct((6, NODE_DEV), f32),
        ),
        in_specs=[vm] * 8,
        out_specs=(vm, vm),
        scratch_shapes=[
            pltpu.VMEM((planes_all * pitch, LANES), f32),
            pltpu.VMEM((planes_all, rows, LANES), jnp.bfloat16),
            pltpu.VMEM((planes_all, rows, LANES), jnp.bfloat16),
            pltpu.VMEM((B * rows, LANES), f32),
            pltpu.VMEM((10, NJ + 2 * SUB, NK), f32),
            pltpu.VMEM((10, NJ + 2 * SUB, NK), f32),
            pltpu.VMEM(field, f32),
            pltpu.VMEM(field, f32),
            pltpu.VMEM(field, f32),
            pltpu.VMEM(field, f32),
            pltpu.VMEM((2, 2, 2 * SUB, NK), f32),
            pltpu.VMEM((2, 2, 2 * SUB, NK), f32),
            pltpu.VMEM((B, SUB, LANES), jnp.int32),
            pltpu.VMEM((B, SUB, LANES), f32),
            dma((B,)), dma((B,)),
            dma((2, 2)), dma((2, 2)),
            dma((2, 2)), dma((2, 2)),
            dma((B,)), dma((B,)),
            dma((B,)), dma((B,)),
        ],
        compiler_params=pltpu.CompilerParams(collective_id=0, has_side_effects=True),
        name="flutter",
    )(jac_blocks[0], psi_start[0, :, 0], source[0, :, 0], pseudo_step[0, 0], dissipation[0, 0],
      freq_volume[0, 0], face_normals, ids)
    return adj[None, :, None], sens[None]


def solution(mesh):
    placed = (
        P("passage", None, None, "brick"),
        P("passage", None, "brick", None, None),
        P("passage", None, "brick", None, None),
        P("passage", "brick", None, None),
        P("passage", "brick", None, None),
        P("passage", "brick", None, None),
        P("passage", None, "brick", None),
        P("passage", "brick", None),
        P("passage", "brick"),
    )
    return jax.shard_map(
        functools.partial(body, mesh.shape["brick"], mesh.shape["passage"]),
        mesh=mesh,
        in_specs=placed,
        out_specs=(P("passage", None, "brick", None, None), P("passage", None, "brick")),
        check_vma=False,
    )
```

time: 128 us -> 41.9 us (0.33)
  waiting for transfers between devices: 84.5 us -> 0 us
  Pallas kernels: 0 us -> 36 us
  starting transfers between devices: 20.1 us -> 0 us
  between operations: 14.5 us -> 0.67 us
  other arithmetic: 4.52 us -> 0.61 us
    reduce_scatter x1 -> x0, waiting for transfers between devices: 68 us -> none  [body(): lax.psum_scatter(local_terms, 'brick', scatter_dimension=1, tiled=True)]
    pallas_call x0 -> x1, Pallas kernels: none -> 36 us  [body(): pl.pallas_call(functools.partial(kernel, B, passes, phase_angle), out_sha...]
    all_to_all x1 -> x0, waiting for transfers between devices: 13.9 us -> none  [body(): lax.all_to_all(jac_blocks, 'brick', split_axis=2, concat_axis=3, tiled=True)]
    ppermute x8 -> x0, starting transfers between devices: 11.2 us -> none  [the longest x4 7.99 us: padded(): before = lax.ppermute(last, axis, up)]
    all_to_all x1 -> x0, starting transfers between devices: 8.92 us -> none  [body(): lax.all_to_all(jac_blocks, 'brick', split_axis=2, concat_axis=3, tiled=True)]
    ppermute x8 -> x0, waiting for transfers between devices: 2.59 us -> none  [the longest x4 2.58 us: padded(): after = lax.ppermute(initial, axis, down)]
    scatter-add x1 -> x0, other arithmetic: 2.23 us -> none  [body(): jnp.zeros((6, NODE_DEV * bricks), jnp.float32).at[:, node_ids].add(values)]
    convert_element_type x2 -> x0, other arithmetic: 1.3 us -> none  [advance(): state.astype(jnp.bfloat16)]
  transfers between devices with their start and end apart: 10 -> 0, of which waited for: 4 -> 0; matrix products, arithmetic and copies ran while one was open for 3% -> 0% of each run, Pallas kernels for 0% -> 0%
where the time goes in v1:
time: 41.9 us; the launch traced here: 41.6 us
  Pallas kernels  36 us (86%)
  local copies, waits for them, and re-layouts  4.3 us (10%)
  between operations  0.67 us (2%)
  other arithmetic  0.61 us (1%)
    pallas_call x1, Pallas kernels, body(): pl.pallas_call(functools.partial(kernel, B, passes, phase_angle), out_sha...  36 us
    unnamed x9, local copies, waits for them, and re-layouts  3.7 us

profile of v1, /device:TPU:0, one launch (start us, length us, event | category | flops | bytes accessed | tf_op | source)
XLA Modules:
  0.0 41.6 jit_solution(11934327931784615137)
XLA Ops:
  0.6 0.0 copy-start.1
  0.6 0.0 copy-start.2
  0.7 0.0 copy-start
  0.7 0.6 %copy-done.1 = s32[1,64]{1,0:T(1,128)S(1)} copy-done((s32[1,64]{1,0:T(1,128)S(1)}, s32[1,64]{1,0:T(1,128)}, u32[]{:S(2)}) %copy-start.1) | copy-done | bytes 280
  1.3 0.0 copy-done.2
  1.3 0.0 copy-done
  1.3 0.6 %select_maximum_fusion.normals = f32[8,128]{1,0:T(8,128)} fusion(f32[3,64]{1,0:T(4,128)S(1)} %bitcast.22), kind=kLoop, calls=%fused_computation | loop fusion | flops 8192 | bytes 4864 | tf_op jit(solution)/shard_map/concatenate | solution.py:274
  1.9 0.6 %pad.9.ids = s32[8,128]{1,0:T(8,128)} pad(s32[1,64]{1,0:T(1,128)S(1)} %bitcast_add_fusion, s32[]{:T(128)} %constant.6.clone.1), padding=0_7x0_64 | pad | bytes 4356 | tf_op jit(solution)/shard_map/jit(_pad)/pad | solution.py:272
  2.5 36.0 %flutter.1 = (f32[10,64,128]{2,1,0:T(8,128)}, f32[6,256]{1,0:T(8,128)}) custom-call(bf16[25,16,512]{2,1,0:T(8,128)(2,1)} %bitcast.15, f32[10,64,128]{2,1,0:T(8,128)} %bitcast.17, f32[10,64,128]{2,1,0:T(8,128)} %bitcast.18, f32[64,128]{1,0:T(8,128)} %bitcast.19, f32[64,128]{1,0:T(8,128)} %bitcast.20, f32[64,128]{1,0:T(8,128)} %bitcast.21, ...), custom_call_target="tpu_custom_call" | custom-call | tf_op jit(solution)/shard_map/flutter/pallas_call | solution.py:281
  38.6 1.3 %copy.12 = f32[1,6,256]{2,0,1:T(1,128)} copy(f32[1,6,256]{2,1,0:T(8,128)} %bitcast.23) | data formatting | bytes 12288
  39.9 1.7 %copy.17 = f32[1,10,1,64,128]{4,3,2,1,0:T(8,128)} copy(f32[1,10,1,64,128]{4,3,2,1,0:T(8,128)} %bitcast.16) | data formatting | bytes 655360
  (2 shorter events, 0.0 us)
Async XLA Ops:
  0.6 0.7 %copy-start.1 = (s32[1,64]{1,0:T(1,128)S(1)}, s32[1,64]{1,0:T(1,128)}, u32[]{:S(2)}) copy-start(s32[1,64]{1,0:T(1,128)} %param.17) | copy-start | bytes 772
  0.6 0.7 %copy-start.2 = (s32[1,64,1]{1,2,0:T(1,128)S(1)}, s32[1,64,1]{1,2,0:T(1,128)}, u32[]{:S(2)}) copy-start(s32[1,64,1]{1,2,0:T(1,128)} %param.16) | copy-start | bytes 772
  0.7 0.7 %copy-start = (f32[1,3,1,64]{3,2,1,0:T(1,128)S(1)}, f32[1,3,1,64]{3,2,1,0:T(1,128)}, u32[]{:S(2)}) copy-start(f32[1,3,1,64]{3,2,1,0:T(1,128)} %param.15) | copy-start | bytes 2308

commit v2 on v1

--- a/solution.py
+++ b/solution.py
@@ -14,6 +14,8 @@
 BLADES = 36
 LANES = 128
 SUB = 8
+CODE = 32767.0
+BOUND = 6.0
 MESH = pl.DeviceIdType.MESH
 
 
@@ -24,15 +26,17 @@
 
 def kernel(
     B, passes, phase_angle,
-    jac, psi, source, pstep, diss, freq, normals, ids,
-    adj, sens,
-    jpack, jsend, jrecv, jflat, pad0, pad1, low0, high0, low1, high1,
+    jac_h, psi_h, source_h, pstep_h, diss_h, freq_h, normals_h, owner_h, slot_h,
+    adj_h, sens,
+    jac, source, pstep, diss, freq, normals_v, owner, slot, adj, normals, ids,
+    jpack, jsend, jrecv, jflat, pad0, pad1, low, high,
+    code0, low0, high0, code1, low1, high1, scale1, low_scale, high_scale,
     rim_send, rim_recv, idbuf, valbuf,
-    j_s, j_r, h_s, h_r, r_s, r_r, i_s, i_r, v_s, v_r,
+    l_s, o_s, j_s, j_r, h_s, h_r, c_s, c_r, r_s, r_r, i_s, i_r, v_s, v_r,
 ):
     me = lax.axis_index("brick")
     mp = lax.axis_index("passage")
-    NJ, NK = psi.shape[1], psi.shape[2]
+    NJ, NK = source.shape[1], source.shape[2]
     R = jac.shape[2] // LANES
     planes = jac.shape[1]
     rows = 25 * R
@@ -52,6 +56,30 @@
         pl.semaphore_signal(barrier, inc=1, device_id={"passage": down_p}, device_id_type=MESH)
         greeted += 1
 
+    psi = pad0.at[:, pl.ds(SUB, NJ), :]
+    loads = [
+        pltpu.make_async_copy(src, dst, l_s.at[k])
+        for k, (src, dst) in enumerate((
+            (jac_h, jac), (psi_h, psi), (owner_h, owner), (slot_h, slot), (normals_h, normals_v),
+            (source_h, source), (pstep_h, pstep), (diss_h, diss), (freq_h, freq),
+        ))
+    ]
+    for load in loads:
+        load.start()
+
+    @pl.when(me == 0)
+    def _():
+        low0[...] = jnp.zeros_like(low0)
+        low1[...] = jnp.zeros_like(low1)
+        low_scale[...] = jnp.zeros_like(low_scale)
+
+    @pl.when(me == B - 1)
+    def _():
+        high0[...] = jnp.zeros_like(high0)
+        high1[...] = jnp.zeros_like(high1)
+        high_scale[...] = jnp.zeros_like(high_scale)
+
+    loads[0].wait()
     for n in range(25):
         for r in range(R):
             for g in range(planes // SUB):
@@ -78,7 +106,7 @@
             for k, peer in ((0, up_p), (1, down_p))
         ]
 
-    def halo_copies(sweep, src, low, high):
+    def halo_copies(h_s, h_r, sweep, src, low, high):
         up = pltpu.make_async_remote_copy(
             src_ref=src, dst_ref=low, send_sem=h_s.at[sweep, 0], recv_sem=h_r.at[sweep, 0],
             device_id={"brick": lax.rem(me + 1, B)}, device_id_type=MESH,
@@ -98,22 +126,14 @@
         def _():
             down.start()
 
-    def halo_recv(up, down, low, high):
+    def halo_recv(up, down):
         @pl.when(me > 0)
         def _():
             up.wait_recv()
 
-        @pl.when(me == 0)
-        def _():
-            low[...] = jnp.zeros_like(low)
-
         @pl.when(me < B - 1)
         def _():
             down.wait_recv()
-
-        @pl.when(me == B - 1)
-        def _():
-            high[...] = jnp.zeros_like(high)
 
     def halo_sent(up, down):
         @pl.when(me < B - 1)
@@ -124,7 +144,16 @@
         def _():
             down.wait_send()
 
-    fill_rims(0, psi, 0, NJ - 1)
+    loads[1].wait()
+    fill_rims(0, pad0, SUB, SUB + NJ - 1)
+    for c in range(10):
+        q = jnp.round(pad0[c, pl.ds(SUB, NJ), :] * (CODE / BOUND))
+        code0[c, :, :] = q.astype(jnp.int32).astype(jnp.int16)
+    loads[2].wait()
+    loads[3].wait()
+    faces = owner.shape[1]
+    ids[...] = jnp.full((SUB, LANES), -1, jnp.int32)
+    ids[0:1, pl.ds(0, faces)] = owner[...] * NODE_DEV + slot[...]
     idbuf[pl.ds(me, 1), :, :] = ids[...].reshape(1, SUB, LANES)
 
     j_copies, id_copies, val_copies = [], [], []
@@ -140,9 +169,9 @@
             src_ref=valbuf.at[me], dst_ref=valbuf.at[me], send_sem=v_s.at[k], recv_sem=v_r.at[k],
             device_id={"brick": peer}, device_id_type=MESH))
     rims0, rims1 = rim_copies(0), rim_copies(1)
-    halo0 = halo_copies(0, psi, low0, high0)
-    inner = pad1.at[:, pl.ds(SUB, NJ), :]
-    halo1 = halo_copies(1, inner, low1, high1)
+    halo0 = halo_copies(h_s, h_r, 0, code0, low0, high0)
+    halo1 = halo_copies(h_s, h_r, 1, code1, low1, high1)
+    scales = halo_copies(c_s, c_r, 0, scale1, low_scale, high_scale)
 
     pl.semaphore_wait(barrier, greeted)
     for copy in j_copies:
@@ -154,8 +183,12 @@
         copy.start()
 
     jrecv[pl.ds(me, 1), :, :] = jsend[pl.ds(me, 1), :, :]
-    for c in range(10):
-        pad0[c, pl.ds(SUB, NJ), :] = psi[c, :, :]
+    for load in loads[4:]:
+        load.wait()
+    normals[...] = jnp.zeros_like(normals)
+    for d in range(3):
+        for k in (d, 3 + d):
+            normals[pl.ds(k, 1), pl.ds(0, faces)] = normals_v[d, :, :]
 
     lane = lax.broadcasted_iota(jnp.int32, (SUB, NK), 1)
 
@@ -204,22 +237,37 @@
     for copy in rims0:
         copy.wait_recv()
     place_rims(0, pad0)
-    halo_recv(*halo0, low0, high0)
+    halo_recv(*halo0)
+    for code, field in ((low0, low), (high0, high)):
+        for c in range(10):
+            field[c, :, :] = code[c, :, :].astype(jnp.int32).astype(jnp.float32) * (BOUND / CODE)
     for copy in j_copies:
         copy.wait_recv()
     for s in range(B):
         jflat[pl.ds(s * rows, rows), :] = jrecv[s, :, :].astype(jnp.float32)
 
-    advance(pad0, low0, high0, pad1, SUB)
+    advance(pad0, low, high, pad1, SUB)
     fill_rims(1, pad1, SUB, SUB + NJ - 1)
+    for copy in rims1:
+        copy.start()
+    for c in range(10):
+        x = pad1[c, pl.ds(SUB, NJ), :]
+        top = jnp.maximum(jnp.max(jnp.abs(x), axis=0, keepdims=True), 1e-30)
+        scale1[pl.ds(c, 1), :] = top * (1.0 / CODE)
+        code1[c, :, :] = jnp.round(x * (CODE / top)).astype(jnp.int32).astype(jnp.int16)
+    halo_start(*scales)
     halo_start(*halo1)
-    for copy in rims1:
-        copy.start()
     for copy in rims1:
         copy.wait_recv()
     place_rims(1, pad1)
-    halo_recv(*halo1, low1, high1)
-    advance(pad1, low1, high1, adj, 0)
+    halo_recv(*scales)
+    halo_recv(*halo1)
+    for code, scale, field in ((low1, low_scale, low), (high1, high_scale, high)):
+        for c in range(10):
+            f = code[c, :, :].astype(jnp.int32).astype(jnp.float32)
+            field[c, :, :] = f * scale[pl.ds(c, 1), :]
+    advance(pad1, low, high, adj, 0)
+    store = pltpu.make_async_copy(adj, adj_h, o_s)
 
     lanes = lax.broadcasted_iota(jnp.int32, (NJ, NK), 1)
     wall = jnp.zeros((NJ, NK), jnp.float32)
@@ -234,6 +282,7 @@
     valbuf[pl.ds(me, 1), :, :] = values.reshape(1, SUB, LANES)
     for copy in val_copies:
         copy.start()
+    store.start()
 
     for copy in id_copies:
         copy.wait_recv()
@@ -252,12 +301,30 @@
             parts, hit, (((1,), (1,)), ((), ())), preferred_element_type=jnp.float32
         )
     summed = total[0:SUB] + total[SUB : 2 * SUB] + total[2 * SUB :]
-    sens[...] = summed[0:6]
+    sens[...] = summed[0:6].reshape(6, 1, NODE_DEV)
+    store.wait()
 
     for copy in j_copies + id_copies + val_copies + rims0 + rims1:
         copy.wait_send()
     halo_sent(*halo0)
     halo_sent(*halo1)
+    halo_sent(*scales)
+
+
+def hand_over(adj, sens, adj_out, sens_out, adj_v, sens_v, in_s, out_s):
+    parts = [(sens, sens_v, sens_out)]
+    for k in range(5):
+        at = pl.ds(2 * k, 2)
+        parts.append((adj.at[at], adj_v.at[at], adj_out.at[at]))
+    ins = [pltpu.make_async_copy(a, v, in_s.at[k]) for k, (a, v, _) in enumerate(parts)]
+    outs = [pltpu.make_async_copy(v, o, out_s.at[k]) for k, (_, v, o) in enumerate(parts)]
+    for copy in ins:
+        copy.start()
+    for arrive, leave in zip(ins, outs):
+        arrive.wait()
+        leave.start()
+    for copy in outs:
+        copy.wait()
 
 
 def body(B, passes, jac_blocks, psi_start, source, pseudo_step, dissipation, freq_volume,
@@ -268,25 +335,33 @@
     R = cells // LANES
     rows = 25 * R
     pitch = -(-rows // SUB) * SUB
-    node_ids = face_owner[:, :, 0] * NODE_DEV + face_slot
-    ids = jnp.pad(node_ids, ((0, SUB - 1), (0, LANES - node_ids.shape[1])), constant_values=-1)
-    face_normals = normals[0, :, 0, :]
-    face_normals = jnp.concatenate([face_normals, face_normals], axis=0)
-    face_normals = jnp.pad(
-        face_normals, ((0, SUB - 6), (0, LANES - face_normals.shape[1])))
+    faces = face_slot.shape[1]
     f32 = jnp.float32
-    field = (10, NJ, NK)
+    i16 = jnp.int16
+    field, plane = (10, NJ, NK), (NJ, NK)
+    hbm = pl.BlockSpec(memory_space=pl.ANY)
     vm = pl.BlockSpec(memory_space=pltpu.VMEM)
     dma = pltpu.SemaphoreType.DMA
     adj, sens = pl.pallas_call(
         functools.partial(kernel, B, passes, phase_angle),
         out_shape=(
             jax.ShapeDtypeStruct(field, f32),
-            jax.ShapeDtypeStruct((6, NODE_DEV), f32),
+            jax.ShapeDtypeStruct((6, 1, NODE_DEV), f32),
         ),
-        in_specs=[vm] * 8,
-        out_specs=(vm, vm),
+        in_specs=[hbm] * 9,
+        out_specs=(hbm, vm),
         scratch_shapes=[
+            pltpu.VMEM((25, planes_all, cells), jnp.bfloat16),
+            pltpu.VMEM(field, f32),
+            pltpu.VMEM(plane, f32),
+            pltpu.VMEM(plane, f32),
+            pltpu.VMEM(plane, f32),
+            pltpu.VMEM((3, 1, faces), f32),
+            pltpu.VMEM((1, faces), jnp.int32),
+            pltpu.VMEM((1, faces), jnp.int32),
+            pltpu.VMEM(field, f32),
+            pltpu.VMEM((SUB, LANES), f32),
+            pltpu.VMEM((SUB, LANES), jnp.int32),
             pltpu.VMEM((planes_all * pitch, LANES), f32),
             pltpu.VMEM((planes_all, rows, LANES), jnp.bfloat16),
             pltpu.VMEM((planes_all, rows, LANES), jnp.bfloat16),
@@ -295,14 +370,23 @@
             pltpu.VMEM((10, NJ + 2 * SUB, NK), f32),
             pltpu.VMEM(field, f32),
             pltpu.VMEM(field, f32),
-            pltpu.VMEM(field, f32),
-            pltpu.VMEM(field, f32),
+            pltpu.VMEM(field, i16),
+            pltpu.VMEM(field, i16),
+            pltpu.VMEM(field, i16),
+            pltpu.VMEM(field, i16),
+            pltpu.VMEM(field, i16),
+            pltpu.VMEM(field, i16),
+            pltpu.VMEM((2 * SUB, NK), f32),
+            pltpu.VMEM((2 * SUB, NK), f32),
+            pltpu.VMEM((2 * SUB, NK), f32),
             pltpu.VMEM((2, 2, 2 * SUB, NK), f32),
             pltpu.VMEM((2, 2, 2 * SUB, NK), f32),
             pltpu.VMEM((B, SUB, LANES), jnp.int32),
             pltpu.VMEM((B, SUB, LANES), f32),
+            dma((9,)), dma,
             dma((B,)), dma((B,)),
             dma((2, 2)), dma((2, 2)),
+            dma((1, 2)), dma((1, 2)),
             dma((2, 2)), dma((2, 2)),
             dma((B,)), dma((B,)),
             dma((B,)), dma((B,)),
@@ -310,8 +394,23 @@
         compiler_params=pltpu.CompilerParams(collective_id=0, has_side_effects=True),
         name="flutter",
     )(jac_blocks[0], psi_start[0, :, 0], source[0, :, 0], pseudo_step[0, 0], dissipation[0, 0],
-      freq_volume[0, 0], face_normals, ids)
-    return adj[None, :, None], sens[None]
+      freq_volume[0, 0], normals[0], face_owner[:, :, 0], face_slot)
+    adj, sens = pl.pallas_call(
+        hand_over,
+        out_shape=(
+            jax.ShapeDtypeStruct(field, f32),
+            jax.ShapeDtypeStruct((6, 1, NODE_DEV), f32),
+        ),
+        in_specs=[hbm, hbm],
+        out_specs=(hbm, hbm),
+        scratch_shapes=[
+            pltpu.VMEM(field, f32),
+            pltpu.VMEM((6, 1, NODE_DEV), f32),
+            dma((6,)), dma((6,)),
+        ],
+        name="hand_over",
+    )(adj, sens)
+    return adj[None, :, None], jnp.transpose(sens, (1, 0, 2))
 
 
 def solution(mesh):

time: 41.9 us -> 33.2 us (0.79)
  local copies, waits for them, and re-layouts: 4.3 us -> 0 us
  Pallas kernels: 36 us -> 32.4 us
  other arithmetic: 0.61 us -> 0 us
    pallas_call x1, Pallas kernels: 36 us -> 30.7 us  [body(): pl.pallas_call(functools.partial(kernel, B, passes, phase_angle), out_sha...]
    unnamed x9 -> x0, local copies, waits for them, and re-layouts: 3.7 us -> none
    pallas_call x0 -> x1, Pallas kernels: none -> 1.72 us  [body(): pl.pallas_call(hand_over, out_shape=(jax.ShapeDtypeStruct(field, f32), ja...]
    concatenate x1 -> x0, other arithmetic: 0.6 us -> none  [body(): face_normals = jnp.concatenate([face_normals, face_normals], axis=0)]
    pad x1 -> x0, local copies, waits for them, and re-layouts: 0.6 us -> none  [body(): jnp.pad(node_ids, ((0, SUB - 1), (0, LANES - node_ids.shape[1])), constan...]
where the time goes in v2:
time: 33.2 us; the launch traced here: 33 us
  Pallas kernels  32.4 us (98%)
  between operations  0.64 us (2%)
    pallas_call x1, Pallas kernels, body(): pl.pallas_call(functools.partial(kernel, B, passes, phase_angle), out_sha...  30.7 us
    pallas_call x1, Pallas kernels, body(): pl.pallas_call(hand_over, out_shape=(jax.ShapeDtypeStruct(field, f32), ja...  1.72 us

profile of v2, /device:TPU:0, one launch (start us, length us, event | category | flops | bytes accessed | tf_op | source)
XLA Modules:
  0.0 33.0 jit_solution(3122233766081515137)
XLA Ops:
  0.6 30.7 %flutter.1 = (f32[10,64,128]{2,1,0:T(8,128)}, f32[6,1,256]{2,1,0:T(1,128)}) custom-call(bf16[25,16,512]{2,1,0:T(8,128)(2,1)} %bitcast.12, f32[10,64,128]{2,1,0:T(8,128)} %bitcast.13, f32[10,64,128]{2,1,0:T(8,128)} %bitcast.14, f32[64,128]{1,0:T(8,128)} %bitcast.15, f32[64,128]{1,0:T(8,128)} %bitcast.16, f32[64,128]{1,0:T(8,128)} %bitcast.17, ...), custom_call_target="tpu_custom_call" | custom-call | tf_op jit(solution)/shard_map/flutter/pallas_call | solution.py:345
  31.3 1.7 %hand_over.1 = (f32[10,64,128]{2,1,0:T(8,128)}, f32[6,1,256]{2,1,0:T(1,128)}) custom-call(f32[10,64,128]{2,1,0:T(8,128)} %get-tuple-element.6.adj, f32[6,1,256]{2,1,0:T(1,128)} %get-tuple-element.7.sens), custom_call_target="tpu_custom_call" | custom-call | tf_op jit(solution)/shard_map/hand_over/pallas_call | solution.py:398

commit v3 on v2

--- a/solution.py
+++ b/solution.py
@@ -19,11 +19,6 @@
 MESH = pl.DeviceIdType.MESH
 
 
-def far_first(count):
-    half = count // 2
-    return sorted(range(1, count), key=lambda d: (abs(d - half), d))
-
-
 def kernel(
     B, passes, phase_angle,
     jac_h, psi_h, source_h, pstep_h, diss_h, freq_h, normals_h, owner_h, slot_h,
@@ -31,8 +26,8 @@
     jac, source, pstep, diss, freq, normals_v, owner, slot, adj, normals, ids,
     jpack, jsend, jrecv, jflat, pad0, pad1, low, high,
     code0, low0, high0, code1, low1, high1, scale1, low_scale, high_scale,
-    rim_send, rim_recv, idbuf, valbuf,
-    l_s, o_s, j_s, j_r, h_s, h_r, c_s, c_r, r_s, r_r, i_s, i_r, v_s, v_r,
+    rim_send, rim_recv, idbuf, valbuf, hits, turned, wall_send, low_wall, high_wall, rim_wall,
+    l_s, o_s, j_s, j_r, h_s, h_r, c_s, c_r, w_s, w_r, r_s, r_r, i_s, i_r, v_s, v_r,
 ):
     me = lax.axis_index("brick")
     mp = lax.axis_index("passage")
@@ -41,7 +36,7 @@
     planes = jac.shape[1]
     rows = 25 * R
     pitch = jpack.shape[0] // planes
-    others = far_first(B)
+    others = range(1, B)
     up_p = lax.rem(mp + 1, passes)
     down_p = lax.rem(mp + passes - 1, passes)
 
@@ -72,12 +67,14 @@
         low0[...] = jnp.zeros_like(low0)
         low1[...] = jnp.zeros_like(low1)
         low_scale[...] = jnp.zeros_like(low_scale)
+        low_wall[...] = jnp.zeros_like(low_wall)
 
     @pl.when(me == B - 1)
     def _():
         high0[...] = jnp.zeros_like(high0)
         high1[...] = jnp.zeros_like(high1)
         high_scale[...] = jnp.zeros_like(high_scale)
+        high_wall[...] = jnp.zeros_like(high_wall)
 
     loads[0].wait()
     for n in range(25):
@@ -171,16 +168,17 @@
     rims0, rims1 = rim_copies(0), rim_copies(1)
     halo0 = halo_copies(h_s, h_r, 0, code0, low0, high0)
     halo1 = halo_copies(h_s, h_r, 1, code1, low1, high1)
+    walls = halo_copies(w_s, w_r, 0, wall_send, low_wall, high_wall)
     scales = halo_copies(c_s, c_r, 0, scale1, low_scale, high_scale)
 
     pl.semaphore_wait(barrier, greeted)
+    for copy in id_copies:
+        copy.start()
     for copy in j_copies:
         copy.start()
     for copy in rims0:
         copy.start()
     halo_start(*halo0)
-    for copy in id_copies:
-        copy.start()
 
     jrecv[pl.ds(me, 1), :, :] = jsend[pl.ds(me, 1), :, :]
     for load in loads[4:]:
@@ -202,6 +200,9 @@
             cosine = jnp.where(at_edge, math.cos(turn), 1.0).astype(jnp.float32)
             sine = jnp.where(at_edge, math.sin(turn), 0.0).astype(jnp.float32)
             re, im = re * cosine - im * sine, re * sine + im * cosine
+            if sweep == SWEEPS - 1:
+                rim_wall[k, 0:5, :] = re
+                rim_wall[k, SUB : SUB + 5, :] = im
             for c in range(5):
                 pad[c, pl.ds(row, 1), :] = re[c : c + 1]
                 pad[5 + c, pl.ds(row, 1), :] = im[c : c + 1]
@@ -234,6 +235,26 @@
                 resid = conv[c] + spin + ds_ * (6.0 * u - beside) - source[c, at, :]
                 out[c, pl.ds(shift + t * SUB, SUB), :] = u - ps * resid
 
+    lanes = lax.broadcasted_iota(jnp.int32, (NJ, NK), 1)
+
+    def turn_over(slot, pieces):
+        packed = jnp.zeros((NJ, NK), jnp.float32)
+        for to, column, x in pieces:
+            shift = (to - column) % NK
+            x = pltpu.roll(x, shift, 1) if shift else x
+            packed = jnp.where(lanes == to, x, packed)
+        if NJ < LANES:
+            packed = jnp.concatenate([packed, jnp.zeros((LANES - NJ, NK), jnp.float32)], axis=0)
+        turned[slot, :, :] = packed.T
+
+    turn_over(0, [(0, 0, pstep[...]), (1, 0, diss[...]), (2, 0, freq[...])]
+              + [(SUB + c + c // 5 * 3, 0, source[c, :, :]) for c in range(10)])
+    for copy in id_copies:
+        copy.wait_recv()
+    node = lax.broadcasted_iota(jnp.int32, (NODE_DEV, LANES), 0) + me * NODE_DEV
+    for s in range(B):
+        hits[s, :, :] = jnp.where(idbuf[s, 0:1, :] == node, 1.0, 0.0).astype(jnp.bfloat16)
+
     for copy in rims0:
         copy.wait_recv()
     place_rims(0, pad0)
@@ -250,6 +271,11 @@
     fill_rims(1, pad1, SUB, SUB + NJ - 1)
     for copy in rims1:
         copy.start()
+    turn_over(2, [
+        (16 * k + c + c // 5 * 3, k, pad1[c, pl.ds(SUB, NJ), :]) for k in range(2) for c in range(10)
+    ])
+    wall_send[...] = turned[2, 0:16, :]
+    halo_start(*walls)
     for c in range(10):
         x = pad1[c, pl.ds(SUB, NJ), :]
         top = jnp.maximum(jnp.max(jnp.abs(x), axis=0, keepdims=True), 1e-30)
@@ -260,6 +286,33 @@
     for copy in rims1:
         copy.wait_recv()
     place_rims(1, pad1)
+    turn_over(1, [
+        (SUB * n + m, 0, jflat[pl.ds(n * 5 + m, NJ, stride=25), :])
+        for n in range(5) for m in range(5)
+    ])
+    halo_recv(*walls)
+    face = lax.broadcasted_iota(jnp.int32, (5, LANES), 1)
+    sides = normals[0:3, :]
+    valbuf[pl.ds(me, 1), :, :] = jnp.zeros((1, SUB, LANES), jnp.float32)
+    for part in range(2):
+        at = pl.ds(SUB * part, 5)
+        u, lo, hi = turned[2, at, :], low_wall[at, :], high_wall[at, :]
+        diff = 0.5 * (hi - lo)
+        conv = turned[1, 0:5, :] * diff[0:1]
+        for n in range(1, 5):
+            conv = conv + turned[1, pl.ds(SUB * n, 5), :] * diff[n : n + 1]
+        below = jnp.where(face == 0, rim_wall[0, at, :][:, 0:1], pltpu.roll(u, 1, 1))
+        above = jnp.where(face == NJ - 1, rim_wall[1, at, :][:, 0:1], pltpu.roll(u, LANES - 1, 1))
+        beside = hi + lo + above + below + turned[2, pl.ds(16 + SUB * part, 5), :]
+        spin = turned[0, 2:3, :] * turned[2, pl.ds(SUB * (1 - part), 5), :]
+        spin = -spin if part else spin
+        resid = conv + spin + turned[0, 1:2, :] * (6.0 * u - beside)
+        resid = resid - turned[0, pl.ds(SUB + SUB * part, 5), :]
+        fresh = u - turned[0, 0:1, :] * resid
+        valbuf[pl.ds(me, 1), pl.ds(3 * part, 3), :] = (fresh[1:4] * sides)[None]
+    for copy in val_copies:
+        copy.start()
+
     halo_recv(*scales)
     halo_recv(*halo1)
     for code, scale, field in ((low1, low_scale, low), (high1, high_scale, high)):
@@ -269,36 +322,19 @@
     advance(pad1, low, high, adj, 0)
     store = pltpu.make_async_copy(adj, adj_h, o_s)
 
-    lanes = lax.broadcasted_iota(jnp.int32, (NJ, NK), 1)
-    wall = jnp.zeros((NJ, NK), jnp.float32)
-    for k, c in enumerate((1, 2, 3, 6, 7, 8)):
-        column = adj[c, :, :]
-        if k:
-            column = pltpu.roll(column, k, 1)
-        wall = jnp.where(lanes == k, column, wall)
-    if NJ < LANES:
-        wall = jnp.concatenate([wall, jnp.zeros((LANES - NJ, NK), jnp.float32)], axis=0)
-    values = wall.T[0:SUB] * normals[...]
-    valbuf[pl.ds(me, 1), :, :] = values.reshape(1, SUB, LANES)
-    for copy in val_copies:
-        copy.start()
     store.start()
 
-    for copy in id_copies:
-        copy.wait_recv()
     for copy in val_copies:
         copy.wait_recv()
-    node = lax.broadcasted_iota(jnp.int32, (NODE_DEV, LANES), 0) + me * NODE_DEV
     total = jnp.zeros((3 * SUB, NODE_DEV), jnp.float32)
     for s in range(B):
-        hit = jnp.where(idbuf[s, 0:1, :] == node, 1.0, 0.0).astype(jnp.bfloat16)
         v = valbuf[s, :, :]
         a = v.astype(jnp.bfloat16).astype(jnp.float32)
         rest = v - a
         b = rest.astype(jnp.bfloat16).astype(jnp.float32)
         parts = jnp.concatenate([a, b, rest - b], axis=0).astype(jnp.bfloat16)
         total = total + lax.dot_general(
-            parts, hit, (((1,), (1,)), ((), ())), preferred_element_type=jnp.float32
+            parts, hits[s, :, :], (((1,), (1,)), ((), ())), preferred_element_type=jnp.float32
         )
     summed = total[0:SUB] + total[SUB : 2 * SUB] + total[2 * SUB :]
     sens[...] = summed[0:6].reshape(6, 1, NODE_DEV)
@@ -309,6 +345,7 @@
     halo_sent(*halo0)
     halo_sent(*halo1)
     halo_sent(*scales)
+    halo_sent(*walls)
 
 
 def hand_over(adj, sens, adj_out, sens_out, adj_v, sens_v, in_s, out_s):
@@ -383,9 +420,16 @@
             pltpu.VMEM((2, 2, 2 * SUB, NK), f32),
             pltpu.VMEM((B, SUB, LANES), jnp.int32),
             pltpu.VMEM((B, SUB, LANES), f32),
+            pltpu.VMEM((B, NODE_DEV, LANES), jnp.bfloat16),
+            pltpu.VMEM((3, NK, LANES), f32),
+            pltpu.VMEM((2 * SUB, LANES), f32),
+            pltpu.VMEM((2 * SUB, LANES), f32),
+            pltpu.VMEM((2 * SUB, LANES), f32),
+            pltpu.VMEM((2, 2 * SUB, LANES), f32),
             dma((9,)), dma,
             dma((B,)), dma((B,)),
             dma((2, 2)), dma((2, 2)),
+            dma((1, 2)), dma((1, 2)),
             dma((1, 2)), dma((1, 2)),
             dma((2, 2)), dma((2, 2)),
             dma((B,)), dma((B,)),

time: 33.2 us -> 32.2 us (0.970)
  Pallas kernels: 32.4 us -> 31.3 us
    pallas_call x1, Pallas kernels: 30.7 us -> 29.6 us  [body(): pl.pallas_call(functools.partial(kernel, B, passes, phase_angle), out_sha...]
where the time goes in v3:
time: 32.2 us; the launch traced here: 32 us
  Pallas kernels  31.3 us (97%)
  between operations  0.64 us (2%)
    pallas_call x1, Pallas kernels, body(): pl.pallas_call(functools.partial(kernel, B, passes, phase_angle), out_sha...  29.6 us
    pallas_call x1, Pallas kernels, body(): pl.pallas_call(hand_over, out_shape=(jax.ShapeDtypeStruct(field, f32), ja...  1.72 us

profile of v3, /device:TPU:0, one launch (start us, length us, event | category | flops | bytes accessed | tf_op | source)
XLA Modules:
  0.0 32.0 jit_solution(2119600905653804847)
XLA Ops:
  0.6 29.6 %flutter.1 = (f32[10,64,128]{2,1,0:T(8,128)}, f32[6,1,256]{2,1,0:T(1,128)}) custom-call(bf16[25,16,512]{2,1,0:T(8,128)(2,1)} %bitcast.12, f32[10,64,128]{2,1,0:T(8,128)} %bitcast.13, f32[10,64,128]{2,1,0:T(8,128)} %bitcast.14, f32[64,128]{1,0:T(8,128)} %bitcast.15, f32[64,128]{1,0:T(8,128)} %bitcast.16, f32[64,128]{1,0:T(8,128)} %bitcast.17, ...), custom_call_target="tpu_custom_call" | custom-call | tf_op jit(solution)/shard_map/flutter/pallas_call | solution.py:382
  30.3 1.7 %hand_over.1 = (f32[10,64,128]{2,1,0:T(8,128)}, f32[6,1,256]{2,1,0:T(1,128)}) custom-call(f32[10,64,128]{2,1,0:T(8,128)} %get-tuple-element.6.adj, f32[6,1,256]{2,1,0:T(1,128)} %get-tuple-element.7.sens), custom_call_target="tpu_custom_call" | custom-call | tf_op jit(solution)/shard_map/hand_over/pallas_call | solution.py:442

commit v4 on v3

--- a/solution.py
+++ b/solution.py
@@ -220,7 +220,7 @@
             conv = [None] * 10
             for n in range(5):
                 for m in range(5):
-                    tile = jflat[pl.ds(t * SUB * 25 + n * 5 + m, SUB, stride=25), :]
+                    tile = jflat[pl.ds(t * SUB * step + n * 5 + m, SUB, stride=step), :]
                     for part in (0, 5):
                         term = tile * diff[part + n]
                         conv[part + m] = term if conv[part + m] is None else conv[part + m] + term
@@ -255,6 +255,19 @@
     for s in range(B):
         hits[s, :, :] = jnp.where(idbuf[s, 0:1, :] == node, 1.0, 0.0).astype(jnp.bfloat16)
 
+    step = jflat.shape[0] // NJ
+
+    def unpack(s):
+        x = jrecv[pl.ds(s, 1), :, :].reshape(rows, LANES).astype(jnp.float32)
+        base = pl.multiple_of(s * (R * step), SUB)
+        for r in range(R):
+            jflat[pl.ds(base + r * step, 25), :] = x[r * 25 : r * 25 + 25]
+
+    unpack(me)
+    for d, copy in zip(others, j_copies):
+        copy.wait_recv()
+        unpack(lax.rem(me + B - d, B))
+
     for copy in rims0:
         copy.wait_recv()
     place_rims(0, pad0)
@@ -262,11 +275,6 @@
     for code, field in ((low0, low), (high0, high)):
         for c in range(10):
             field[c, :, :] = code[c, :, :].astype(jnp.int32).astype(jnp.float32) * (BOUND / CODE)
-    for copy in j_copies:
-        copy.wait_recv()
-    for s in range(B):
-        jflat[pl.ds(s * rows, rows), :] = jrecv[s, :, :].astype(jnp.float32)
-
     advance(pad0, low, high, pad1, SUB)
     fill_rims(1, pad1, SUB, SUB + NJ - 1)
     for copy in rims1:
@@ -281,13 +289,11 @@
         top = jnp.maximum(jnp.max(jnp.abs(x), axis=0, keepdims=True), 1e-30)
         scale1[pl.ds(c, 1), :] = top * (1.0 / CODE)
         code1[c, :, :] = jnp.round(x * (CODE / top)).astype(jnp.int32).astype(jnp.int16)
-    halo_start(*scales)
-    halo_start(*halo1)
     for copy in rims1:
         copy.wait_recv()
     place_rims(1, pad1)
     turn_over(1, [
-        (SUB * n + m, 0, jflat[pl.ds(n * 5 + m, NJ, stride=25), :])
+        (SUB * n + m, 0, jflat[pl.ds(n * 5 + m, NJ, stride=step), :])
         for n in range(5) for m in range(5)
     ])
     halo_recv(*walls)
@@ -312,6 +318,8 @@
         valbuf[pl.ds(me, 1), pl.ds(3 * part, 3), :] = (fresh[1:4] * sides)[None]
     for copy in val_copies:
         copy.start()
+    halo_start(*scales)
+    halo_start(*halo1)
 
     halo_recv(*scales)
     halo_recv(*halo1)
@@ -373,6 +381,7 @@
     rows = 25 * R
     pitch = -(-rows // SUB) * SUB
     faces = face_slot.shape[1]
+    step = next(k for k in range(25, 33) if R * k % SUB == 0)
     f32 = jnp.float32
     i16 = jnp.int16
     field, plane = (10, NJ, NK), (NJ, NK)
@@ -402,7 +411,7 @@
             pltpu.VMEM((planes_all * pitch, LANES), f32),
             pltpu.VMEM((planes_all, rows, LANES), jnp.bfloat16),
             pltpu.VMEM((planes_all, rows, LANES), jnp.bfloat16),
-            pltpu.VMEM((B * rows, LANES), f32),
+            pltpu.VMEM((NJ * step, LANES), f32),
             pltpu.VMEM((10, NJ + 2 * SUB, NK), f32),
             pltpu.VMEM((10, NJ + 2 * SUB, NK), f32),
             pltpu.VMEM(field, f32),

time: 32.2 us -> 32.2 us (level)
  no operation moved by 1% of the time
where the time goes in v4:
time: 32.2 us; the launch traced here: 31.9 us
  Pallas kernels  31.2 us (97%)
  between operations  0.64 us (2%)
    pallas_call x1, Pallas kernels, body(): pl.pallas_call(functools.partial(kernel, B, passes, phase_angle), out_sha...  29.5 us
    pallas_call x1, Pallas kernels, body(): pl.pallas_call(hand_over, out_shape=(jax.ShapeDtypeStruct(field, f32), ja...  1.72 us

profile of v4, /device:TPU:0, one launch (start us, length us, event | category | flops | bytes accessed | tf_op | source)
XLA Modules:
  0.0 31.9 jit_solution(5471427444983942699)
XLA Ops:
  0.6 29.5 %flutter.1 = (f32[10,64,128]{2,1,0:T(8,128)}, f32[6,1,256]{2,1,0:T(1,128)}) custom-call(bf16[25,16,512]{2,1,0:T(8,128)(2,1)} %bitcast.12, f32[10,64,128]{2,1,0:T(8,128)} %bitcast.13, f32[10,64,128]{2,1,0:T(8,128)} %bitcast.14, f32[64,128]{1,0:T(8,128)} %bitcast.15, f32[64,128]{1,0:T(8,128)} %bitcast.16, f32[64,128]{1,0:T(8,128)} %bitcast.17, ...), custom_call_target="tpu_custom_call" | custom-call | tf_op jit(solution)/shard_map/flutter/pallas_call | solution.py:391
  30.1 1.7 %hand_over.1 = (f32[10,64,128]{2,1,0:T(8,128)}, f32[6,1,256]{2,1,0:T(1,128)}) custom-call(f32[10,64,128]{2,1,0:T(8,128)} %get-tuple-element.6.adj, f32[6,1,256]{2,1,0:T(1,128)} %get-tuple-element.7.sens), custom_call_target="tpu_custom_call" | custom-call | tf_op jit(solution)/shard_map/hand_over/pallas_call | solution.py:451
